TPU v7x, 32 devices: a whole 2x2x4 slice. The times are simulated.
32 devices in a mesh: grp: 2 (over core), dp: 4 (over y, x), sp: 4 (over z).
Axes of the slice: x: 2, y: 2, z: 4, core: 2. Of those that a mesh axis runs over, the one named last changes fastest.
Arguments:
- vis: bfloat16 [512, 5120], P(('grp', 'dp', 'sp')), may hold values from -6 to 6
- merge_weight: bfloat16 [5120, 8192], P('dp', ('grp', 'sp')), may hold values from -0.078125 to 0.078125
- img_counts: int32 [32], P('dp'), may hold values from 1 to 16
- img_pos: int32 [512], P(('grp', 'dp', 'sp')), may hold values from 0 to 127, as said below
- text: bfloat16 [4096, 8192], P(('grp', 'dp', 'sp')), may hold values from -6 to 6
- cot: bfloat16 [4096, 8192], P(('grp', 'dp', 'sp')), may hold values from -6 to 6
- gain: float32 [8192], replicated, may hold values from 0.25 to 1.75
Outputs:
- vis_grad: bfloat16 [512, 5120], P(('grp', 'dp', 'sp'))
- gain_grad: float32 [8192], replicated
Inputs may be any that keep to these rules, and one draw needn't show every extreme that they name: `img_pos`: within one device's block the 16 positions are distinct. `img_counts`: the counts of one image group sum to at most 128.
All inputs are finite; a program needn't handle non-finite values.
Results may differ from a plain program's by a relative error of at most 0.014.
Values may be sent and summed in bfloat16 or wider, within the bound.
No kernel may reach another device: no remote copies, remote signals or barrier semaphores. Data moves between devices by JAX's collectives and lax.ppermute only.
A program may use at most 128 MiB of HBM per device.

v0:
```python
import jax
import jax.numpy as jnp
from jax import lax
from jax.sharding import PartitionSpec as P


def body(vis, merge_weight, img_counts, img_pos, text, cot, gain):
    rows_dev = vis.shape[0]
    tok_rows = text.shape[0]
    group_vis = lax.all_gather(vis, ("grp", "sp"), axis=0, tiled=True)
    full_weight = lax.all_gather(merge_weight, "dp", axis=0, tiled=True)
    partial_value = jnp.dot(group_vis, full_weight, preferred_element_type=jnp.float32)
    emb = lax.all_to_all(
        partial_value.astype(jnp.bfloat16), ("grp", "sp"), split_axis=0, concat_axis=1, tiled=True
    )
    total_live = jnp.sum(img_counts)
    member = lax.axis_index("grp") * lax.axis_size("sp") + lax.axis_index("sp")
    group_row = member * rows_dev + jnp.arange(rows_dev, dtype=jnp.int32)
    live = group_row < total_live
    places = jnp.arange(tok_rows, dtype=jnp.int32)
    select = (img_pos[None, :] == places[:, None]) & live[None, :]
    taken = jnp.any(select, axis=1)
    select_b = select.astype(jnp.bfloat16)
    placed = jnp.dot(select_b, emb, preferred_element_type=jnp.float32)
    hidden = jnp.where(taken[:, None], placed, text.astype(jnp.float32))
    rinv = lax.rsqrt(jnp.mean(hidden * hidden, axis=1, keepdims=True) + 1e-06)
    cotf = cot.astype(jnp.float32)
    part_gain = jnp.sum(cotf * hidden * rinv, axis=0)
    scaled = cotf * gain[None, :]
    inner = jnp.mean(scaled * hidden, axis=1, keepdims=True)
    dhid = (rinv * scaled - hidden * rinv**3 * inner).astype(jnp.bfloat16)
    demb = jnp.dot(select_b.T, dhid, preferred_element_type=jnp.float32)
    demb = jnp.where(live[:, None], demb, 0.0).astype(jnp.bfloat16)
    returned = lax.all_to_all(demb, ("grp", "sp"), split_axis=1, concat_axis=0, tiled=True)
    terms = lax.dot_general(
        returned, full_weight, (((1,), (1,)), ((), ())), preferred_element_type=jnp.float32
    )
    vis_grad = lax.psum_scatter(
        terms.astype(jnp.bfloat16), ("grp", "sp"), scatter_dimension=0, tiled=True
    )
    gain_grad = lax.psum(part_gain, ("grp", "dp", "sp"))
    return (vis_grad, gain_grad)


def solution(mesh):
    return jax.shard_map(
        body,
        mesh=mesh,
        in_specs=(
            P(("grp", "dp", "sp"), None),
            P("dp", ("grp", "sp")),
            P("dp"),
            P(("grp", "dp", "sp")),
            P(("grp", "dp", "sp"), None),
            P(("grp", "dp", "sp"), None),
            P(),
        ),
        out_specs=(P(("grp", "dp", "sp"), None), P()),
        check_vma=False,
    )
```

profile of v0, /device:TPU:0, one launch (start us, length us, event | category | flops | bytes accessed | tf_op | source)
XLA Modules:
  0.0 229.6 jit_solution(17347707635758896386)
XLA Ops:
  7.2 0.0 all-gather.3.cloned.1.call-start
  7.2 0.7 all-gather.3.cloned.1.call-update
  7.9 0.0 all-gather.5.cloned.1.call-start
  7.9 0.7 all-gather.5.cloned.1.call-update
  8.6 0.0 copy-start.4
  8.7 0.0 copy-start.3
  8.7 0.0 copy-start
  8.7 27.1 %all-gather.3.cloned.1.call-done = bf16[128,5120]{1,0:T(8,128)(2,1)} async-done(((bf16[16,5120]{1,0:T(8,128)(2,1)}), bf16[128,5120]{1,0:T(8,128)(2,1)}) %all-gather.3.cloned.1.call-update) | async-done | bytes 1310736 | tf_op jit(solution)/shard_map/all_gather | solution.py:10
  35.7 106.3 %all-gather.5.cloned.1.call-done = bf16[5120,1024]{1,0:T(8,128)(2,1)} async-done(((bf16[1280,1024]{1,0:T(8,128)(2,1)}), bf16[5120,1024]{1,0:T(8,128)(2,1)}) %all-gather.5.cloned.1.call-update) | async-done | bytes 10485776 | tf_op jit(solution)/shard_map/all_gather | solution.py:11
  142.1 6.6 %convolution_convert_fusion.1 = bf16[128,1024]{1,0:T(8,128)(2,1)} fusion(bf16[128,5120]{1,0:T(8,128)(2,1)} %all-gather.3.cloned.1.call-done, bf16[5120,1024]{1,0:T(8,128)(2,1)} %all-gather.5.cloned.1.call-done), kind=kOutput, calls=%fused_computation.14 | convolution fusion | flops 1342308352 | bytes 12058624 | tf_op jit(solution)/shard_map/dot_general | solution.py:12
  148.7 4.7 %all-to-all-start = ((bf16[8,16,1024]{2,1,0:T(8,128)(2,1)}), bf16[8,16,1024]{2,1,0:T(8,128)(2,1)S(1)}, u32[]{:S(2)}, u32[]{:S(2)}) async-start(bf16[8,16,1024]{2,1,0:T(8,128)(2,1)} %bitcast), calls=%async_computation | async-start | bytes 524288 | tf_op jit(solution)/shard_map/all_to_all | solution.py:13
  153.4 0.0 reduce-scatter.2.cloned.1.call-start
  153.5 0.0 copy-done.4
  153.5 0.6 reduce_sum.36
  154.1 0.7 add_compare_fusion
  154.8 0.0 copy-done.3
  154.8 0.1 fusion.12
  154.9 7.9 %all-to-all-done = bf16[8,16,1024]{2,1,0:T(8,128)(2,1)S(1)} async-done(((bf16[8,16,1024]{2,1,0:T(8,128)(2,1)}), bf16[8,16,1024]{2,1,0:T(8,128)(2,1)S(1)}, u32[]{:S(2)}, u32[]{:S(2)}) %all-to-all-start) | async-done | bytes 262176 | tf_op jit(solution)/shard_map/all_to_all | solution.py:13
  162.8 0.0 copy-done
  162.8 0.0 slice-start
  162.8 1.0 multiply_reduce_fusion
  163.8 0.0 copy-done.2
  163.8 0.6 copy-done.1
  164.4 1.5 fusion.7
  165.9 1.1 fusion
  167.1 11.8 %all_to_all.38 = bf16[16,8,1024]{2,0,1:T(8,128)(2,1)S(1)} all-to-all(bf16[16,8,1024]{2,0,1:T(8,128)(2,1)S(1)} %bitcast.21), channel_id=1, replica_groups=mesh['grp'=2,'dp'=4,'sp'=4] {'grp','sp'}, dimensions={1} | all-to-all | bytes 524288 | tf_op jit(solution)/shard_map/all_to_all | solution.py:34
  178.8 0.0 slice-done
  178.9 0.0 slice-done.1
  178.9 0.0 slice-done.2
  178.9 4.6 %convolution_convert_fusion = bf16[128,5120]{1,0:T(8,128)(2,1)} fusion(bf16[128,1024]{1,0:T(8,128)(2,1)S(1)} %bitcast.19, bf16[5120,1024]{1,0:T(8,128)(2,1)S(1)} %bitcast.17), kind=kOutput, calls=%fused_computation.3 | convolution fusion | flops 1342832640 | bytes 12058624 | tf_op jit(solution)/shard_map/dot_general | solution.py:35
  183.5 0.0 reduce-scatter.2.cloned.1.call-update
  183.5 39.5 %psum.7 = f32[8192]{0:T(1024)} all-reduce(f32[8192]{0:T(1024)S(1)} %get-tuple-element.2), channel_id=1, replica_groups=mesh['grp'=2,'dp'=4,'sp'=4] {'grp','dp','sp'}, use_global_device_ids=true, to_apply=%region_6.7 | all-reduce | flops 8192 | bytes 65536 | tf_op jit(solution)/shard_map/psum | solution.py:41
  (10 shorter events, 0.1 us)
Async XLA Ops:
  7.2 28.6 %all-gather.3.cloned.1.call-start = ((), (), s32[]{:S(2)}) async-start(), calls=%async_computation.3 | async-start | bytes 1474560 | tf_op jit(solution)/shard_map/all_gather | solution.py:10
  7.9 134.2 %all-gather.5.cloned.1.call-start = ((), (), s32[]{:S(2)}) async-start(), calls=%async_computation.4 | async-start | bytes 13107200 | tf_op jit(solution)/shard_map/all_gather | solution.py:11
  8.6 144.8 %copy-start.4 = (s32[8]{0:T(128)S(1)}, s32[8]{0:T(128)}, u32[]{:S(2)}) copy-start(s32[8]{0:T(128)} %param.9) | copy-start | bytes 100
  8.7 146.1 %copy-start.3 = (s32[16]{0:T(128)S(1)}, s32[16]{0:T(128)}, u32[]{:S(2)}) copy-start(s32[16]{0:T(128)} %param.10) | copy-start | bytes 196
  8.7 154.1 %copy-start = (bf16[128,8192]{1,0:T(8,128)(2,1)S(1)}, bf16[128,8192]{1,0:T(8,128)(2,1)}, u32[]{:S(2)}) copy-start(bf16[128,8192]{1,0:T(8,128)(2,1)} %param.11) | copy-start | bytes 6291460
  148.7 15.1 %copy-start.2 = (f32[8192]{0:T(1024)S(1)}, f32[8192]{0:T(1024)}, u32[]{:S(2)}) copy-start(f32[8192]{0:T(1024)} %param.13) | copy-start | bytes 98308
  148.7 14.1 %all-to-all-start = ((bf16[8,16,1024]{2,1,0:T(8,128)(2,1)}), bf16[8,16,1024]{2,1,0:T(8,128)(2,1)S(1)}, u32[]{:S(2)}, u32[]{:S(2)}) async-start(bf16[8,16,1024]{2,1,0:T(8,128)(2,1)} %bitcast), calls=%async_computation | async-start | bytes 524288 | tf_op jit(solution)/shard_map/all_to_all | solution.py:13
  153.4 69.6 %reduce-scatter.2.cloned.1.call-start = ((), (), s32[]{:S(2)}) async-start(), calls=%async_computation.5 | async-start | bytes 1474560 | tf_op jit(solution)/shard_map/reduce_scatter | solution.py:38
  162.8 1.6 copy-start.1
  162.8 16.0 %slice-start = ((s8[10485760]{0:T(1024)(128)(4,1)}), s8[4194304]{0:T(1024)(128)(4,1)S(1)}, s32[]{:S(2)}) async-start(s8[10485760]{0:T(1024)(128)(4,1)} %bitcast.16), calls=%async_computation.6 | async-start | bytes 8388608
  164.4 14.5 %slice-start.1 = ((s8[10485760]{0:T(1024)(128)(4,1)}), s8[4194304]{0:T(1024)(128)(4,1)S(1)}, s32[]{:S(2)}) async-start(s8[10485760]{0:T(1024)(128)(4,1)} %bitcast.16), calls=%async_computation.7 | async-start | bytes 8388608
  165.9 13.0 %slice-start.2 = ((s8[10485760]{0:T(1024)(128)(4,1)}), s8[2097152]{0:T(1024)(128)(4,1)S(1)}, s32[]{:S(2)}) async-start(s8[10485760]{0:T(1024)(128)(4,1)} %bitcast.16), calls=%async_computation.8 | async-start | bytes 4194304
Sparse Core Ops, SparseCore 0:
  9.6 26.1 all-gather.2
  37.6 104.4 all-gather.4
  183.6 34.8 reduce-scatter.1
where the time goes:
time: 230 us
  waiting for transfers between devices  143 us (62%)
  blocking collectives  51.3 us (22%)
  between operations  13.9 us (6%)
  matrix products  13.4 us (6%)
  starting transfers between devices  4.85 us (2%)
  other arithmetic  2.91 us (1%)
    all_gather x1, waiting for transfers between devices, body(): full_weight = lax.all_gather(merge_weight, 'dp', axis=0, tiled=True)  106 us
    psum x1, blocking collectives, body(): gain_grad = lax.psum(part_gain, ('grp', 'dp', 'sp'))  39.5 us
    all_gather x1, waiting for transfers between devices, body(): group_vis = lax.all_gather(vis, ('grp', 'sp'), axis=0, tiled=True)  27.1 us
    all_to_all x1, blocking collectives, body(): lax.all_to_all(demb, ('grp', 'sp'), split_axis=1, concat_axis=0, tiled=True)  11.8 us
    all_to_all x1, waiting for transfers between devices, body(): lax.all_to_all(partial_value.astype(jnp.bfloat16), ('grp', 'sp'), split_a...  7.9 us
    dot_general x1, matrix products, body(): jnp.dot(group_vis, full_weight, preferred_element_type=jnp.float32)  6.62 us
    all_to_all x1, starting transfers between devices, body(): lax.all_to_all(partial_value.astype(jnp.bfloat16), ('grp', 'sp'), split_a...  4.74 us
    dot_general x1, matrix products, body(): lax.dot_general(returned, full_weight, (((1,), (1,)), ((), ())), preferre...  4.62 us
  transfers between devices with their start and end apart: 4, of which 3 were waited for; matrix products, arithmetic and copies ran while one was open for 1% of the time, Pallas kernels for 0%

commit v1 on v0

--- a/solution.py
+++ b/solution.py
@@ -38,7 +38,7 @@
     vis_grad = lax.psum_scatter(
         terms.astype(jnp.bfloat16), ("grp", "sp"), scatter_dimension=0, tiled=True
     )
-    gain_grad = lax.psum(part_gain, ("grp", "dp", "sp"))
+    gain_grad = jnp.sum(lax.all_gather(part_gain, ("grp", "dp", "sp")), axis=0)
     return (vis_grad, gain_grad)
 
 

time: 230 us -> 267 us (1.16)
  waiting for transfers between devices: 143 us -> 208 us
  blocking collectives: 51.3 us -> 12.2 us
  matrix products: 13.4 us -> 19.5 us
  local copies, waits for them, and re-layouts: 0.62 us -> 3.59 us
    psum x1 -> x0, blocking collectives: 39.5 us -> none  [body(): gain_grad = lax.psum(part_gain, ('grp', 'dp', 'sp'))]
    reduce_scatter x1, waiting for transfers between devices: 0.01 us -> 36.9 us  [body(): lax.psum_scatter(terms.astype(jnp.bfloat16), ('grp', 'sp'), scatter_dimen...]
    all_gather x0 -> x1, waiting for transfers between devices: none -> 28.4 us  [body(): gain_grad = jnp.sum(lax.all_gather(part_gain, ('grp', 'dp', 'sp')), axis=0)]
    dot_general x1, matrix products: 4.62 us -> 8.63 us  [body(): lax.dot_general(returned, full_weight, (((1,), (1,)), ((), ())), preferre...]
  transfers between devices with their start and end apart: 4 -> 5, of which waited for: 3 -> 5; matrix products, arithmetic and copies ran while one was open for 1% -> 6% of each run, Pallas kernels for 0% -> 0%
where the time goes in v1:
time: 267 us; the launch traced here: 266 us
  waiting for transfers between devices  208 us (78%)
  matrix products  19.5 us (7%)
  between operations  13.9 us (5%)
  blocking collectives  12.2 us (5%)
  starting transfers between devices  4.89 us (2%)
  other arithmetic  4.12 us (2%)
  local copies, waits for them, and re-layouts  3.59 us (1%)
    all_gather x1, waiting for transfers between devices, body(): full_weight = lax.all_gather(merge_weight, 'dp', axis=0, tiled=True)  106 us
    reduce_scatter x1, waiting for transfers between devices, body(): lax.psum_scatter(terms.astype(jnp.bfloat16), ('grp', 'sp'), scatter_dimen...  36.9 us
    all_gather x1, waiting for transfers between devices, body(): gain_grad = jnp.sum(lax.all_gather(part_gain, ('grp', 'dp', 'sp')), axis=0)  28.4 us
    all_gather x1, waiting for transfers between devices, body(): group_vis = lax.all_gather(vis, ('grp', 'sp'), axis=0, tiled=True)  27.1 us
    all_to_all x1, blocking collectives, body(): lax.all_to_all(demb, ('grp', 'sp'), split_axis=1, concat_axis=0, tiled=True)  12.2 us
    dot_general x1, matrix products, body(): lax.dot_general(returned, full_weight, (((1,), (1,)), ((), ())), preferre...  8.63 us
    all_to_all x1, waiting for transfers between devices, body(): lax.all_to_all(partial_value.astype(jnp.bfloat16), ('grp', 'sp'), split_a...  7.9 us
    dot_general x1, matrix products, body(): jnp.dot(group_vis, full_weight, preferred_element_type=jnp.float32)  6.62 us
  transfers between devices with their start and end apart: 5, of which 5 were waited for; matrix products, arithmetic and copies ran while one was open for 6% of the time, Pallas kernels for 0%

profile of v1, /device:TPU:0, one launch (start us, length us, event | category | flops | bytes accessed | tf_op | source)
XLA Modules:
  0.0 266.1 jit_solution(14880978807388212725)
XLA Ops:
  7.2 0.0 all-gather.5.cloned.1.call-start
  7.2 0.7 all-gather.5.cloned.1.call-update
  7.9 0.0 all-gather.7.cloned.1.call-start
  7.9 0.7 all-gather.7.cloned.1.call-update
  8.6 0.0 copy-start.6
  8.7 0.0 copy-start.5
  8.7 0.0 copy-start.1
  8.7 27.1 %all-gather.5.cloned.1.call-done = bf16[128,5120]{1,0:T(8,128)(2,1)} async-done(((bf16[16,5120]{1,0:T(8,128)(2,1)}), bf16[128,5120]{1,0:T(8,128)(2,1)}) %all-gather.5.cloned.1.call-update) | async-done | bytes 1310736 | tf_op jit(solution)/shard_map/all_gather | solution.py:10
  35.7 106.3 %all-gather.7.cloned.1.call-done = bf16[5120,1024]{1,0:T(8,128)(2,1)} async-done(((bf16[1280,1024]{1,0:T(8,128)(2,1)}), bf16[5120,1024]{1,0:T(8,128)(2,1)}) %all-gather.7.cloned.1.call-update) | async-done | bytes 10485776 | tf_op jit(solution)/shard_map/all_gather | solution.py:11
  142.1 6.6 %convolution_convert_fusion.1 = bf16[128,1024]{1,0:T(8,128)(2,1)} fusion(bf16[128,5120]{1,0:T(8,128)(2,1)} %all-gather.5.cloned.1.call-done, bf16[5120,1024]{1,0:T(8,128)(2,1)} %all-gather.7.cloned.1.call-done), kind=kOutput, calls=%fused_computation.14 | convolution fusion | flops 1342308352 | bytes 12058624 | tf_op jit(solution)/shard_map/dot_general | solution.py:12
  148.7 4.7 %all-to-all-start = ((bf16[8,16,1024]{2,1,0:T(8,128)(2,1)}), bf16[8,16,1024]{2,1,0:T(8,128)(2,1)S(1)}, u32[]{:S(2)}, u32[]{:S(2)}) async-start(bf16[8,16,1024]{2,1,0:T(8,128)(2,1)} %bitcast), calls=%async_computation | async-start | bytes 524288 | tf_op jit(solution)/shard_map/all_to_all | solution.py:13
  153.4 0.0 all-gather.9.cloned.1.call-start
  153.5 0.0 copy-done.6
  153.5 0.6 reduce_sum.45
  154.1 0.7 add_compare_fusion
  154.8 0.1 fusion.12
  154.9 7.9 %all-to-all-done = bf16[8,16,1024]{2,1,0:T(8,128)(2,1)S(1)} async-done(((bf16[8,16,1024]{2,1,0:T(8,128)(2,1)}), bf16[8,16,1024]{2,1,0:T(8,128)(2,1)S(1)}, u32[]{:S(2)}, u32[]{:S(2)}) %all-to-all-start) | async-done | bytes 262176 | tf_op jit(solution)/shard_map/all_to_all | solution.py:13
  162.8 0.0 copy-done.1
  162.8 1.0 multiply_reduce_fusion
  163.8 0.0 copy-start.3
  163.8 2.1 copy-done
  165.9 2.0 fusion.7
  168.0 0.0 all-gather.9.cloned.1.call-update
  168.0 0.0 reduce-scatter.2.cloned.1.call-start
  168.1 3.3 %fusion = bf16[16,8192]{1,0:T(8,128)(2,1)S(1)} fusion(bf16[128,8192]{1,0:T(8,128)(2,1)S(1)} %copy-done.3, f32[128,8192]{1,0:T(8,128)} %copy-done, f32[128]{0:T(128)S(1)} %broadcast_multiply_fusion, f32[128]{0:T(128)S(1)} %get-tuple-element.4, f32[8192]{0:T(1024)S(1)} %copy-done.4, f32[128]{0:T(128)S(1)} %get-tuple-element.5, ...), kind=kOutput, calls=%fused_computation.2 | convolution fusion | flops 41160704 | bytes 6587984 | tf_op jit(solution)/shard_map/dot_general | solution.py:32
  171.3 12.2 %all_to_all.38 = bf16[16,8,1024]{2,0,1:T(8,128)(2,1)S(1)} all-to-all(bf16[16,8,1024]{2,0,1:T(8,128)(2,1)S(1)} %bitcast.19), channel_id=1, replica_groups=mesh['grp'=2,'dp'=4,'sp'=4] {'grp','sp'}, dimensions={1} | all-to-all | bytes 524288 | tf_op jit(solution)/shard_map/all_to_all | solution.py:34
  183.5 8.6 %convolution_convert_fusion = bf16[128,5120]{1,0:T(8,128)(2,1)} fusion(bf16[128,1024]{1,0:T(8,128)(2,1)S(1)} %bitcast.17, bf16[5120,1024]{1,0:T(8,128)(2,1)} %all-gather.7.cloned.1.call-done), kind=kOutput, calls=%fused_computation.3 | convolution fusion | flops 1342832640 | bytes 12058624 | tf_op jit(solution)/shard_map/dot_general | solution.py:35
  192.2 0.0 reduce-scatter.2.cloned.1.call-update
  192.2 28.4 %all-gather.9.cloned.1.call-done = f32[262144]{0:T(1024)} async-done(((f32[8192]{0:T(1024)}), f32[262144]{0:T(1024)}) %all-gather.9.cloned.1.call-update) | async-done | bytes 1048592 | tf_op jit(solution)/shard_map/all_gather | solution.py:41
  220.6 1.4 reshape.41
  222.0 0.7 reduce_sum.49
  222.7 36.9 %reduce-scatter.2.cloned.1.call-done = bf16[16,5120]{1,0:T(8,128)(2,1)} async-done(((bf16[128,5120]{1,0:T(8,128)(2,1)}), bf16[16,5120]{1,0:T(8,128)(2,1)}) %reduce-scatter.2.cloned.1.call-update) | async-done | bytes 163856 | tf_op jit(solution)/shard_map/reduce_scatter | solution.py:38
  (11 shorter events, 0.1 us)
Async XLA Ops:
  7.2 28.6 %all-gather.5.cloned.1.call-start = ((), (), s32[]{:S(2)}) async-start(), calls=%async_computation.3 | async-start | bytes 1474560 | tf_op jit(solution)/shard_map/all_gather | solution.py:10
  7.9 134.2 %all-gather.7.cloned.1.call-start = ((), (), s32[]{:S(2)}) async-start(), calls=%async_computation.4 | async-start | bytes 13107200 | tf_op jit(solution)/shard_map/all_gather | solution.py:11
  8.6 144.8 %copy-start.6 = (s32[8]{0:T(128)S(1)}, s32[8]{0:T(128)}, u32[]{:S(2)}) copy-start(s32[8]{0:T(128)} %param.9) | copy-start | bytes 100
  8.7 146.1 %copy-start.5 = (s32[16]{0:T(128)S(1)}, s32[16]{0:T(128)}, u32[]{:S(2)}) copy-start(s32[16]{0:T(128)} %param.10) | copy-start | bytes 196
  8.7 154.1 %copy-start.1 = (bf16[128,8192]{1,0:T(8,128)(2,1)S(1)}, bf16[128,8192]{1,0:T(8,128)(2,1)}, u32[]{:S(2)}) copy-start(bf16[128,8192]{1,0:T(8,128)(2,1)} %param.11) | copy-start | bytes 6291460
  148.7 17.2 %copy-start.4 = (f32[8192]{0:T(1024)S(1)}, f32[8192]{0:T(1024)}, u32[]{:S(2)}) copy-start(f32[8192]{0:T(1024)} %param.13) | copy-start | bytes 98308
  148.7 14.1 %all-to-all-start = ((bf16[8,16,1024]{2,1,0:T(8,128)(2,1)}), bf16[8,16,1024]{2,1,0:T(8,128)(2,1)S(1)}, u32[]{:S(2)}, u32[]{:S(2)}) async-start(bf16[8,16,1024]{2,1,0:T(8,128)(2,1)} %bitcast), calls=%async_computation | async-start | bytes 524288 | tf_op jit(solution)/shard_map/all_to_all | solution.py:13
  153.4 67.1 %all-gather.9.cloned.1.call-start = ((), (), s32[]{:S(2)}) async-start(), calls=%async_computation.6 | async-start | bytes 1081344 | tf_op jit(solution)/shard_map/all_gather | solution.py:41
  162.8 3.1 %copy-start.2 = (bf16[128,8192]{1,0:T(8,128)(2,1)S(1)}, bf16[128,8192]{1,0:T(8,128)(2,1)}, u32[]{:S(2)}) copy-start(bf16[128,8192]{1,0:T(8,128)(2,1)} %param.12) | copy-start | bytes 6291460
  163.8 2.1 copy-start
  163.8 4.3 %copy-start.3 = (bf16[128,8192]{1,0:T(8,128)(2,1)S(1)}, bf16[128,8192]{1,0:T(8,128)(2,1)}, u32[]{:S(2)}) copy-start(bf16[128,8192]{1,0:T(8,128)(2,1)} %param.12) | copy-start | bytes 6291460
  168.0 91.6 %reduce-scatter.2.cloned.1.call-start = ((), (), s32[]{:S(2)}) async-start(), calls=%async_computation.5 | async-start | bytes 1474560 | tf_op jit(solution)/shard_map/reduce_scatter | solution.py:38
Sparse Core Ops, SparseCore 0:
  9.6 26.1 all-gather.4
  37.6 104.4 all-gather.6
  168.1 52.4 all-gather.8
  223.3 36.2 reduce-scatter.1
